TPU v7x, 128 devices: a whole 4x4x4 slice. The times are simulated.
128 devices in a mesh: cluster: 4 (over y), sub: 32 (over x, z, core).
Axes of the slice: x: 4, y: 4, z: 4, core: 2. Of those that a mesh axis runs over, the one named last changes fastest.
Arguments:
- factor_tiles: float32 [128, 300, 128, 128], P(('cluster', 'sub')), may hold values from -1 to 2, as said below
- rigid_modes: float32 [128, 6, 3072], P(('cluster', 'sub')), may hold values from -6 to 6
- load_cases: float32 [128, 32, 3072], P(('cluster', 'sub')), may hold values from -6 to 6
- coarse_load: float32 [24, 32], replicated, may hold values from -20480 to 20480
- peer_slots: int32 [128, 128, 96], P(('cluster', 'sub')), may hold values from 0 to 640, as said below
- slot_unknown: int32 [128, 640], P(('cluster', 'sub')), may hold values from 0 to 3072, as said below
Outputs:
- multipliers: float32 [128, 640, 32], P(('cluster', 'sub'))
- projected: float32 [128, 640, 32], P(('cluster', 'sub'))
Inputs may be any that keep to these rules, and one draw needn't show every extreme that they name: For k below the number of multipliers shared by subdomains a and b, peer_slots[a, b, k] is the slot of a holding the k-th of them, in the same order as peer_slots[b, a, k]; other places hold 640; each slot is listed at most once in peer_slots[a]; a shares multipliers only with the subdomain of the same index within the next or previous cluster (at most 96) and with subdomains of its own cluster whose grid positions differ from its own by at most one in each coordinate, where index w within a cluster stands at z = w // (32 / 2), x = (w % (32 / 2)) // 4, y = w % 4; such a pair shares at most 96 multipliers if the positions differ in one coordinate, at most 12 if in two, at most 3 if in three; some pair shares exactly 96, some pair differing in two coordinates exactly 12. `slot_unknown`: distinct over the listed slots of one subdomain; exactly 3072 on the slots that peer_slots[s] does not list, and every subdomain has such slots. `factor_tiles`: tiles with I = J are lower triangular with diagonal entries from 1 to 2.
All inputs are finite; a program needn't handle non-finite values.
Results may differ from a plain program's by a relative error of at most 0.0003.
Values sent between devices are 32-bit elements; how exact they have to be, the bound alone decides.
No kernel may reach another device: no remote copies, remote signals or barrier semaphores. Data moves between devices by JAX's collectives and lax.ppermute only.
A program may use at most 320 MiB of HBM per device.

v0:
```python
import functools

import jax
import jax.numpy as jnp
from jax import lax
from jax.experimental import pallas as pl
from jax.experimental.pallas import tpu as pltpu
from jax.sharding import PartitionSpec as P

F32 = jnp.float32
BF16 = jnp.bfloat16
HIGH = lax.Precision.HIGHEST

UNKNOWNS = 3072
SLOTS = 640
LOADS = 32
RHS = SLOTS + LOADS
TILE = 128
TILE_ROWS = 24
BLOCK = 256
BLOCKS = UNKNOWNS // BLOCK
SUBS = 32
CLUSTERS = 4
MODES = 6
COARSE = CLUSTERS * MODES
ROWS = LOADS + COARSE
LANES = 128
COARSE_AT = 96
FACES = [(0, 0, 1), (0, 0, -1), (0, 1, 0), (0, -1, 0), (1, 0, 0)]
EDGES = [(0, 1, 1), (0, 1, -1), (1, 0, 1), (1, 1, 0), (1, 1, 1), (1, 1, -1)]
SLOT, EDGE_MOST = 16, 12
LOWER, UPPER, EDGE = len(FACES), len(FACES) + 1, len(FACES) + 2
PLACES = len(FACES) + 4
SMALL = 1 << 22
CHUNK = 12
CHUNKS = 25
STEP = 128
GROUP = 4
VMEM = pl.BlockSpec(memory_space=pltpu.VMEM)
SMEM = pl.BlockSpec(memory_space=pltpu.SMEM)
ANY = pl.BlockSpec(memory_space=pl.ANY)


def nt(a, b, precision=None):
    return lax.dot_general(
        a, b, (((1,), (1,)), ((), ())), precision=precision, preferred_element_type=F32
    )


def nn(a, b, precision=None):
    return lax.dot_general(
        a, b, (((1,), (0,)), ((), ())), precision=precision, preferred_element_type=F32
    )


def halves(a):
    high = a.astype(BF16)
    return high, (a - high.astype(F32)).astype(BF16)


def thirds(a):
    high = a.astype(BF16).astype(F32)
    rest = a - high
    middle = rest.astype(BF16).astype(F32)
    return jnp.concatenate([high, middle, rest - middle], axis=0).astype(BF16)


def fold(a, rows):
    return a[:rows] + a[rows : 2 * rows] + a[2 * rows :]


def times(dot, high, low, right_high, right_low):
    m = high.shape[0]
    product = dot(jnp.concatenate([high, low], axis=0), right_high)
    return product[:m] + product[m:] + dot(high, right_low)


def mm(a, b):
    return times(nn, *halves(a), *halves(b))


def opposite(offset):
    return (offset[0], -offset[1], -offset[2])


def peer_of(me, offset):
    dz, dx, dy = offset
    z, x, y = me // 16, (me // 4) % 4 + dx, me % 4 + dy
    valid = (x >= 0) & (x < 4) & (y >= 0) & (y < 4)
    return valid, jnp.where(valid, (1 - z if dz else z) * 16 + x * 4 + y, me)


def edges():
    for side in (0, 1):
        for slot, offset in enumerate(EDGES):
            yield side, slot, opposite(offset) if side else offset


def in_slot(shape, slot):
    lane = lax.broadcasted_iota(jnp.int32, shape, 1)
    return (lane >= slot * SLOT) & (lane < slot * SLOT + EDGE_MOST)


def lanes_of(values, place):
    return values[:, place * LANES : (place + 1) * LANES]


def pick(picks, place, wanted):
    slot = lax.broadcasted_iota(jnp.int32, (SLOTS, LANES), 0)
    at = pl.ds(pl.multiple_of(place * LANES, LANES), LANES)
    picks[:, at] = jnp.where(slot == wanted, 1.0, 0.0).astype(BF16)


def select_slots(table, picks):
    def one(place, carry):
        at = pl.ds(pl.multiple_of(place * LANES, LANES), LANES)
        pick(picks, place, table[:1, at])
        return carry

    lax.fori_loop(0, PLACES, one, 0)


def send_values(values, extra, me, picks, to_sub, to_lower, to_upper):
    rows = values.shape[0]
    for peer in range(SUBS):
        to_sub[peer] = extra
    picked = fold(nn(thirds(values), picks[...]), rows)
    for place, offset in enumerate(FACES):
        valid, peer = peer_of(me, offset)

        @pl.when(valid)
        def _():
            to_sub[peer] = lanes_of(picked, place) + extra

    for side, slot, offset in edges():
        valid, peer = peer_of(me, offset)

        @pl.when(valid)
        def _():
            mine = lanes_of(picked, EDGE + side)
            to_sub[peer] = jnp.where(in_slot(mine.shape, slot), mine, extra)

    to_lower[...] = lanes_of(picked, LOWER)
    to_upper[...] = lanes_of(picked, UPPER)


def edge_blocks(me, sub, rows):
    blocks = [jnp.zeros((rows, LANES), F32)] * 2
    for side, slot, offset in edges():
        came = sub[peer_of(me, offset)[1]][:rows]
        blocks[side] = jnp.where(in_slot((rows, LANES), slot), came, blocks[side])
    return blocks


def received_sum(me, picks, sub, lower, upper):
    rows = lower.shape[0]
    pieces = [sub[peer_of(me, offset)[1]] for offset in FACES]
    pieces += [lower[...], upper[...]] + edge_blocks(me, sub, rows)
    return fold(nt(thirds(jnp.concatenate(pieces, axis=1)), picks[...]), rows)


def by_cluster(cluster, parts):
    row = lax.broadcasted_iota(jnp.int32, (LOADS, SLOTS), 0)
    placed = jnp.zeros((LOADS, SLOTS), F32)
    for step, part in parts:
        for mode in range(MODES):
            at = (cluster + step) * MODES + mode
            placed = placed + jnp.where(row == at, part[mode : mode + 1, :], 0.0)
    return placed


def prepare_kernel(
    where, peer_slots, unknown_row, rigid,
    table, sorted_unknown, signs, ranks, counts, half, to_sub, to_lower, to_upper,
    peer_table, picks,
):
    me, cluster = where[0], where[1]
    devices = peer_slots.shape[1]
    listed = jnp.concatenate(
        [
            peer_slots[...].astype(F32),
            jnp.full((LANES - peer_slots.shape[0], devices), float(SLOTS), F32),
        ],
        axis=0,
    )
    peer_table[...] = jnp.transpose(listed).astype(jnp.int32)
    base = cluster * SUBS
    own = base + me

    def wanted_of(valid, row):
        return jnp.where(valid, peer_table[pl.ds(row, 1), :], SLOTS)

    ups = []
    for place, offset in enumerate(FACES):
        valid, peer = peer_of(me, offset)
        pick(picks, place, wanted_of(valid, base + peer))
        ups.append(jnp.full((8, LANES), jnp.where(peer > me, 1.0, -1.0), F32))
    pick(picks, LOWER, wanted_of(own >= SUBS, jnp.maximum(own - SUBS, 0)))
    pick(picks, UPPER, wanted_of(own + SUBS < devices, jnp.minimum(own + SUBS, devices - 1)))
    ups += [jnp.full((8, LANES), -1.0, F32), jnp.full((8, LANES), 1.0, F32)]
    wanted = [jnp.full((1, LANES), SLOTS, jnp.int32)] * 2
    signs_of = [jnp.full((8, LANES), 1.0, F32)] * 2
    for side, slot, offset in edges():
        valid, peer = peer_of(me, offset)
        row = wanted_of(valid, base + peer)
        row = pltpu.roll(row, slot * SLOT, 1) if slot else row
        wanted[side] = jnp.where(in_slot((1, LANES), slot), row, wanted[side])
        signs_of[side] = jnp.where(
            in_slot((8, LANES), slot), jnp.where(peer > me, 1.0, -1.0), signs_of[side]
        )
    pick(picks, EDGE, wanted[0])
    pick(picks, EDGE + 1, wanted[1])
    ups = jnp.concatenate(ups + signs_of, axis=1)
    across = lax.broadcasted_iota(jnp.int32, (1, SLOTS), 1)
    key_row = unknown_row[...] * 1024 + across
    key_column = jnp.transpose(jnp.broadcast_to(key_row.astype(F32), (8, SLOTS)))[:, :1]
    key_column = key_column.astype(jnp.int32)
    rank = jnp.sum(jnp.where(key_column < key_row, 1.0, 0.0), axis=0, keepdims=True)
    rank_int = rank.astype(jnp.int32)
    ranks[...] = rank_int
    row = lax.broadcasted_iota(jnp.int32, (8, SLOTS), 0)
    coarse_rank = jnp.right_shift(rank_int, 8)
    digits = jnp.where(row == 0, coarse_rank, jnp.where(row == 1, rank_int - coarse_rank * 256, 1))
    moved = nn(digits.astype(F32).astype(BF16), picks[...])
    moved = moved[:1] * 256.0 + moved[1:2] + (1.0 - moved[2:3]) * 1024.0
    table[...] = jnp.broadcast_to(moved.astype(jnp.int32), (8, PLACES * LANES))
    sign_row = nt(ups.astype(BF16), picks[...])[:1]
    unknown_float = unknown_row[...].astype(F32)
    for start in range(0, SLOTS, LANES):
        match = lax.broadcasted_iota(jnp.int32, (LANES, SLOTS), 0) + start == rank_int
        at = slice(start, start + LANES)
        sorted_unknown[at] = jnp.sum(
            jnp.where(match, unknown_float, 0.0), axis=1, keepdims=True
        ).astype(jnp.int32)
        signs[at] = jnp.sum(jnp.where(match, sign_row, 0.0), axis=1, keepdims=True)
    for block in range(BLOCKS):
        within = jnp.where(unknown_row[...] < (block + 1) * BLOCK, 1.0, 0.0)
        counts[block] = (jnp.sum(within).astype(jnp.int32) + STEP - 1) // STEP
    select_slots(table, picks)
    own = jnp.zeros((24, SLOTS), F32)
    lane = lax.broadcasted_iota(jnp.int32, (SLOTS, BLOCK), 1)
    for block in range(BLOCKS):
        rows = [rigid[mode, :, block * BLOCK : (block + 1) * BLOCK] for mode in range(MODES)]
        rows = jnp.concatenate(rows + [jnp.zeros((8 - MODES, BLOCK), F32)], axis=0)
        glue = jnp.where(sorted_unknown[...] - block * BLOCK == lane, signs[...], 0.0).astype(BF16)
        own = own + nt(thirds(rows), glue)
    own = fold(own, 8)
    half[...] = own
    send_values(own, jnp.zeros((8, LANES), F32), me, picks, to_sub, to_lower, to_upper)


def invert_diagonal(diag, beside, inverse, high, low):
    base, group, some, many = 32, 8, 12, 12
    lane3 = lax.broadcasted_iota(jnp.int32, (some, group, TILE), 2)
    row = lax.broadcasted_iota(jnp.int32, (some, group, TILE), 1)
    flat_lane = lax.broadcasted_iota(jnp.int32, (some * group, TILE), 1)

    def substitute(step, carry):
        tiles = pl.ds(step * some, some)
        given, solved = [], []
        for g in range(base // group):
            block = jnp.zeros((some, group, TILE), F32)
            for b in range(TILE // base):
                at = b * base + g * group
                block = jnp.where(lane3 // base == b, diag[tiles, at : at + group, :], block)
            given.append(block.reshape(some * group, TILE))
            solved.append(jnp.where(row + g * group == lane3 % base, 1.0, 0.0))
        for k in range(base):
            now, at = k // group, k % group
            column = [None] * (base // group)
            for g in range(now, base // group):
                column[g] = jnp.take_along_axis(
                    given[g], flat_lane // base * base + k, axis=1, mode="promise_in_bounds"
                ).reshape(some, group, TILE)
            pivot = solved[now][:, at : at + 1, :] / column[now][:, at : at + 1, :]
            solved[now] = jnp.where(
                row == at,
                pivot,
                jnp.where(row > at, solved[now] - column[now] * pivot, solved[now]),
            )
            for g in range(now + 1, base // group):
                solved[g] = solved[g] - column[g] * pivot
        for g in range(base // group):
            for b in range(TILE // base):
                at = b * base + g * group
                inverse[tiles, at : at + group, :] = jnp.where(lane3 // base == b, solved[g], 0.0)
        return carry

    lax.fori_loop(0, TILE_ROWS // some, substitute, 0)
    half, quarter = TILE // 2, TILE // 4
    odd = [slice(quarter, half), slice(half + quarter, TILE)]
    lane = lax.broadcasted_iota(jnp.int32, (quarter, TILE), 1)
    none = jnp.zeros((quarter, TILE), F32)

    def merge_quarters(step, carry):
        for n in range(many):
            t = step * many + n
            below = [
                jnp.where(lane < quarter, diag[t, odd[0], :], 0.0),
                jnp.where((lane >= half) & (lane < half + quarter), diag[t, odd[1], :], 0.0),
            ]
            partial = mm(jnp.concatenate(below, axis=0), inverse[t])
            partial = jnp.concatenate([none, partial[:quarter], none, partial[quarter:]], axis=0)
            rows = jnp.concatenate([inverse[t, odd[0], :], inverse[t, odd[1], :]], axis=0)
            rows = rows - mm(rows, partial)
            inverse[t, odd[0], :] = rows[:quarter]
            inverse[t, odd[1], :] = rows[quarter:]
        return carry

    lax.fori_loop(0, TILE_ROWS // many, merge_quarters, 0)

    def merge_halves(step, carry):
        for n in range(many):
            t = step * many + n
            partial = mm(diag[t, half:, :half], inverse[t, :half, :half])
            inverse[t, half:, :half] = -mm(inverse[t, half:, half:], partial)
        return carry

    lax.fori_loop(0, TILE_ROWS // many, merge_halves, 0)

    def merge_tiles(step, carry):
        for n in range(many // 2):
            j = step * (many // 2) + n
            first, second = inverse[2 * j], inverse[2 * j + 1]
            off = -mm(second, mm(beside[j], first))
            whole = jnp.concatenate(
                [
                    jnp.concatenate([first, jnp.zeros((TILE, TILE), F32)], axis=1),
                    jnp.concatenate([off, second], axis=1),
                ],
                axis=0,
            )
            high[j], low[j] = halves(whole)
        return carry

    lax.fori_loop(0, 2 * BLOCKS // many, merge_tiles, 0)


def solve_kernel(
    counts, tiles, unknown, signs, loads, dual, load,
    held, xh, xl, total, diag, beside, inverse, high, low, sems, early_sems,
):
    def copy(c):
        at = pl.ds(c * CHUNK, CHUNK)
        return pltpu.make_async_copy(tiles.at[at], held.at[at], sems.at[c])

    early = []
    for t in range(TILE_ROWS):
        at = t * (t + 1) // 2 + t
        early.append(pltpu.make_async_copy(tiles.at[at], diag.at[t], early_sems.at[t]))
        if t % 2:
            early.append(
                pltpu.make_async_copy(
                    tiles.at[at - 1], beside.at[t // 2], early_sems.at[TILE_ROWS + t // 2]
                )
            )
    for one in early:
        one.start()
    for c in range(CHUNKS):
        copy(c).start()
    dual[...] = jnp.zeros_like(dual)
    load[...] = jnp.zeros_like(load)
    lane = lax.broadcasted_iota(jnp.int32, (SLOTS, BLOCK), 1)
    for i in range(BLOCKS):
        total[i, :LOADS] = loads[:, i * BLOCK : (i + 1) * BLOCK]
        total[i, LOADS:] = jnp.where(unknown[...] - i * BLOCK == lane, signs[...], 0.0)
    for one in early:
        one.wait()
    invert_diagonal(diag, beside, inverse, high, low)
    for c in range(CHUNKS):
        copy(c).wait()

    def block_column(k, carry):
        for c in range(SLOTS // STEP + 1):

            @pl.when(counts[k] == c)
            def _():
                m = LOADS + c * STEP
                ah, al = halves(total[k, :m])
                solved = times(nt, ah, al, high[k], low[k])
                ah, al = halves(solved)
                xh[:m], xl[:m] = ah, al
                if c:
                    product = nt(jnp.concatenate([ah, al, ah], axis=1), jnp.concatenate([ah[LOADS:], ah[LOADS:], al[LOADS:]], axis=1))
                    load[:, : c * STEP] += product[:LOADS]
                    dual[: c * STEP, : c * STEP] += product[LOADS:]

                def update(group, carry):
                    ah, al = xh[:m], xl[:m]
                    for j in range(GROUP):
                        i = BLOCKS - 1 - j - group * GROUP
                        upper = i * (2 * i + 1) + 2 * k
                        under = upper + 2 * i + 1
                        tile = jnp.concatenate(
                            [
                                jnp.concatenate([held[upper], held[upper + 1]], axis=1),
                                jnp.concatenate([held[under], held[under + 1]], axis=1),
                            ],
                            axis=0,
                        )
                        th, tl = halves(tile)
                        total[i, :m] -= times(nt, ah, al, th, tl)
                    return carry

                lax.fori_loop(0, (BLOCKS - 1 - k + GROUP - 1) // GROUP, update, 0)

        return carry

    lax.fori_loop(0, BLOCKS, block_column, 0)


def pack_gram(gram, extra):
    lane = lax.broadcasted_iota(jnp.int32, extra.shape, 1)
    gram = coarse_lanes(gram)
    columns = [pltpu.roll(gram, 24, 1)[:24], pltpu.roll(gram[16:24], 8, 1)]
    columns = jnp.concatenate(columns + [pltpu.roll(gram, 16, 1)[:24]], axis=0)
    return jnp.where(lane >= COARSE_AT + COARSE, columns, coarse_lanes(extra))


def unpack_gram(sums):
    row = lax.broadcasted_iota(jnp.int32, (LOADS, LANES), 0)
    lane = lax.broadcasted_iota(jnp.int32, (LOADS, LANES), 1)
    none = jnp.zeros((8, LANES), F32)
    known = jnp.concatenate([pltpu.roll(sums[LOADS:], 16, 1), none], axis=0)
    known = jnp.where(lane < 8, pltpu.roll(sums[:LOADS], 8, 1), known)
    last = jnp.concatenate([none, none, pltpu.roll(sums[24:LOADS], 24, 1), none], axis=0)
    known = jnp.where(lane < 16, known, jnp.where(row >= 16, last, 0.0))
    known = jnp.where((lane < 24) & (row < 24), known, 0.0)
    turned = nt(jnp.where(row == lane, 1.0, 0.0), known, HIGH)
    turned = jnp.concatenate([turned, jnp.zeros((LOADS, LANES - LOADS), F32)], axis=1)
    return jnp.where((row < 16) & (lane >= 16), turned, known)


def gram_inverse(filled):
    row = lax.broadcasted_iota(jnp.int32, (LOADS, LANES), 0)
    lane = lax.broadcasted_iota(jnp.int32, (LOADS, LANES), 1)
    filled = jnp.where((row >= CLUSTERS * MODES) & (row == lane), 1.0, filled)
    filled = jnp.where(lane == row + LOADS, 1.0, filled)
    for k in range(CLUSTERS * MODES):
        pivot = filled[k : k + 1, :] / filled[k : k + 1, k : k + 1]
        factor = jnp.where(row[:, :1] > k, filled[:, k : k + 1], 0.0)
        filled = filled - factor * pivot
    scale = jnp.sum(jnp.where(row == lane, filled, 0.0), axis=1, keepdims=True)
    lower = jnp.where((lane >= LOADS) & (lane < 2 * LOADS) & (row < CLUSTERS * MODES), filled, 0.0)
    lower = lower * lax.rsqrt(scale)
    lower = pltpu.roll(lower, COARSE_AT - LOADS, 1)
    return lax.dot_general(
        lower, lower, (((0,), (0,)), ((), ())), precision=HIGH, preferred_element_type=F32
    )


def coarse_lanes(values):
    lane = lax.broadcasted_iota(jnp.int32, values.shape, 1)
    return jnp.where((lane >= COARSE_AT) & (lane < COARSE_AT + CLUSTERS * MODES), values, 0.0)


def with_scalars(values, *scalars):
    lane = lax.broadcasted_iota(jnp.int32, values.shape, 1)
    values = coarse_lanes(values)
    for place, scalar in enumerate(scalars):
        values = jnp.where(lane == COARSE_AT + CLUSTERS * MODES + place, scalar, values)
    return values


def scalar(values, place):
    at = COARSE_AT + CLUSTERS * MODES + place
    return values[:, at : at + 1]


def rows_sum(a, b):
    return jnp.sum(a * b, axis=1, keepdims=True)


def start_kernel(
    where, table, half, sub, lower, upper, dual, load,
    modes, values, to_sub, to_lower, to_upper, picks,
):
    select_slots(table, picks)
    me, cluster = where[0], where[1]
    none = jnp.zeros((8, LANES), F32)
    within = [sub[peer_of(me, offset)[1]] for offset in FACES]
    within += [none, none] + edge_blocks(me, sub, 8)
    below = [none] * LOWER + [lower[...]] + [none] * (PLACES - LOWER - 1)
    above = [none] * UPPER + [upper[...]] + [none] * (PLACES - UPPER - 1)
    came = [jnp.concatenate(pieces, axis=1) for pieces in (within, below, above)]
    came = fold(nt(thirds(jnp.concatenate(came, axis=0)), picks[...]), 24)
    total = by_cluster(cluster, [(0, half[...] + came[:8]), (-1, came[8:16]), (1, came[16:])])
    modes[...] = jnp.concatenate([jnp.zeros((COARSE_AT, SLOTS), F32), total], axis=0)
    values[:LOADS] = load[...]
    values[LOADS:] = nn(total, dual[...], HIGH)[:COARSE]
    extra = nt(values[...], modes[...], HIGH)
    extra = pack_gram(0.5 * nt(total, modes[...], HIGH), extra)
    send_values(values[...], extra, me, picks, to_sub, to_lower, to_upper)


def pair_kernel(where, table, values, sub, lower, upper, paired, picks):
    select_slots(table, picks)
    paired[...] = values[...] + received_sum(where[0], picks, sub, lower, upper)


def first_kernel(
    where, table, s0, s1, s2, s3, coarse_load, modes, dual, paired,
    inverse, multipliers, projected, values, to_sub, to_lower, to_upper, picks,
):
    select_slots(table, picks)
    sums = (s0[...] + s1[...]) + (s2[...] + s3[...])
    inverse[...] = gram_inverse(unpack_gram(sums))
    begin = nn(coarse_load[...], inverse[...], HIGH)
    multipliers[...] = nn(begin, modes[...], HIGH)
    images = jnp.concatenate(
        [jnp.zeros((COARSE_AT, SLOTS), F32), paired[LOADS:], jnp.zeros((8, SLOTS), F32)], axis=0
    )
    residual = paired[:LOADS] - nn(begin, images, HIGH)
    sums = coarse_lanes(sums)
    curved = jnp.concatenate(
        [jnp.zeros((COARSE_AT, LANES), F32), sums[LOADS:], jnp.zeros((8, LANES), F32)], axis=0
    )
    weights = nn(sums[:LOADS] - nn(begin, curved, HIGH), inverse[...], HIGH)
    projected[...] = residual - nn(weights, modes[...], HIGH)
    values[...] = nn(projected[...], dual[...], HIGH)
    extra = with_scalars(
        nt(values[...], modes[...], HIGH),
        0.5 * rows_sum(projected[...], projected[...]),
        rows_sum(projected[...], values[...]),
    )
    send_values(values[...], extra, where[0], picks, to_sub, to_lower, to_upper)


def second_kernel(
    where, table, s0, s1, s2, s3, inverse, modes, dual, image, multipliers, projected,
    sums, moved, newer, values, to_sub, to_lower, to_upper, picks,
):
    select_slots(table, picks)
    sums[...] = (s0[...] + s1[...]) + (s2[...] + s3[...])
    alpha = scalar(sums, 0) / scalar(sums, 1)
    weights = nn(coarse_lanes(sums[...]), inverse[...], HIGH)
    moved[...] = multipliers[...] + alpha * projected[...]
    newer[...] = projected[...] - alpha * (image[...] - nn(weights, modes[...], HIGH))
    values[...] = nn(newer[...], dual[...], HIGH)
    extra = with_scalars(
        nt(values[...], modes[...], HIGH),
        0.5 * rows_sum(newer[...], newer[...]),
        rows_sum(newer[...], values[...]),
        0.5 * rows_sum(newer[...], image[...]),
    )
    send_values(values[...], extra, where[0], picks, to_sub, to_lower, to_upper)


def last_kernel(
    s0, s1, s2, s3, before, inverse, modes, paired, image, moved, projected, newer, ranks,
    multipliers_out, projected_out,
):
    sums = (s0[...] + s1[...]) + (s2[...] + s3[...])
    following = scalar(sums, 0)
    beta = following / scalar(before, 0)
    curvature = scalar(sums, 1) + beta * (2.0 * scalar(sums, 2) + beta * scalar(before, 1))
    alpha = following / curvature
    direction = newer[...] + beta * projected[...]
    image_now = paired[...] + beta * image[...]
    coarse = coarse_lanes(sums + beta * before[...])
    weights = nn(coarse, inverse[...], HIGH)
    both = jnp.concatenate(
        [
            moved[...] + alpha * direction,
            newer[...] - alpha * (image_now - nn(weights, modes[...], HIGH)),
        ],
        axis=0,
    )
    back = lax.broadcasted_iota(jnp.int32, (SLOTS, SLOTS), 0) == ranks[...]
    both = fold(nn(thirds(both), jnp.where(back, 1.0, 0.0).astype(BF16)), 2 * LOADS)
    multipliers_out[...] = both[:LOADS]
    projected_out[...] = both[LOADS:]


def shape(*dims, dtype=F32):
    return jax.ShapeDtypeStruct(dims, dtype)


def sent_shapes(rows):
    return (shape(SUBS, rows, LANES), shape(rows, LANES), shape(rows, LANES))


SENT = sent_shapes(LOADS)
VECTOR = shape(LOADS, SLOTS)
PICKS = pltpu.VMEM((SLOTS, PLACES * LANES), BF16)


def call(
    kernel, out_shape, in_specs, scratch, flops, moved, name, limit=24, out_specs=None
):
    return pl.pallas_call(
        kernel,
        out_shape=out_shape,
        in_specs=in_specs,
        out_specs=out_specs or jax.tree.map(lambda _: VMEM, out_shape),
        scratch_shapes=scratch,
        cost_estimate=pl.CostEstimate(flops=flops, bytes_accessed=moved, transcendentals=0),
        compiler_params=pltpu.CompilerParams(vmem_limit_bytes=limit << 20),
        name=name,
    )


def run_solve(counts, tiles, unknown, signs, loads):
    return call(
        solve_kernel,
        (shape(SLOTS, SLOTS), VECTOR),
        [SMEM, ANY] + [VMEM] * 3,
        [
            pltpu.VMEM(tiles.shape, F32),
            pltpu.VMEM((RHS, BLOCK), BF16),
            pltpu.VMEM((RHS, BLOCK), BF16),
            pltpu.VMEM((BLOCKS, RHS, BLOCK), F32),
            pltpu.VMEM((TILE_ROWS, TILE, TILE), F32),
            pltpu.VMEM((BLOCKS, TILE, TILE), F32),
            pltpu.VMEM((TILE_ROWS, TILE, TILE), F32),
            pltpu.VMEM((BLOCKS, BLOCK, BLOCK), BF16),
            pltpu.VMEM((BLOCKS, BLOCK, BLOCK), BF16),
            pltpu.SemaphoreType.DMA((CHUNKS,)),
            pltpu.SemaphoreType.DMA((TILE_ROWS + BLOCKS,)),
        ],
        30 << 30, 5 * SMALL, "solve", 50,
    )(counts, tiles, unknown, signs, loads)


def exchange(sent):
    to_sub, to_lower, to_upper = sent
    up = [(c, c + 1) for c in range(CLUSTERS - 1)]
    down = [(c + 1, c) for c in range(CLUSTERS - 1)]
    from_lower = lax.ppermute(to_upper, "cluster", up)
    from_upper = lax.ppermute(to_lower, "cluster", down)
    received = lax.all_to_all(to_sub, "sub", split_axis=0, concat_axis=0, tiled=True)
    return received, from_lower, from_upper


def cluster_sums(received):
    own = jnp.sum(received, axis=0)
    others = [
        lax.ppermute(own, "cluster", [(c, (c + by) % CLUSTERS) for c in range(CLUSTERS)])
        for by in (1, 2, 3)
    ]
    return (own, *others)


def local(factor_tiles, rigid_modes, load_cases, coarse_load, peer_slots, slot_unknown):
    cluster = lax.axis_index("cluster")
    me = lax.axis_index("sub")
    where = jnp.stack([me, cluster]).astype(jnp.int32)

    table, unknown, signs, ranks, counts, half, *sent = call(
        prepare_kernel,
        (
            shape(8, PLACES * LANES, dtype=jnp.int32),
            shape(SLOTS, 1, dtype=jnp.int32),
            shape(SLOTS, 1),
            shape(1, SLOTS, dtype=jnp.int32),
            shape(16, dtype=jnp.int32),
            shape(8, SLOTS),
            *sent_shapes(8),
        ),
        [SMEM, VMEM, VMEM, VMEM],
        [pltpu.VMEM((CLUSTERS * SUBS, LANES), jnp.int32), PICKS],
        1 << 30, SMALL, "prepare",
        out_specs=(VMEM, VMEM, VMEM, VMEM, SMEM, VMEM, VMEM, VMEM, VMEM),
    )(where, peer_slots[0].T, slot_unknown, jnp.swapaxes(rigid_modes, 0, 1))
    received = exchange(sent)
    dual, load = run_solve(counts, factor_tiles[0], unknown, signs, load_cases[0])

    modes, values, *sent = call(
        start_kernel,
        (shape(LANES, SLOTS), shape(ROWS, SLOTS), *sent_shapes(ROWS)),
        [SMEM] + [VMEM] * 7,
        [PICKS], 1 << 30, SMALL, "start",
    )(where, table, half, *received, dual, load)

    def meet(values, sent):
        received = exchange(sent)
        sums = cluster_sums(received[0])
        paired = call(
            pair_kernel,
            shape(*values.shape),
            [SMEM] + [VMEM] * 5,
            [PICKS], 1 << 30, SMALL, "pair",
        )(where, table, values, *received)
        return sums, paired

    sums, paired = meet(values, sent)
    spread_load = jnp.pad(
        coarse_load.T, ((0, 0), (COARSE_AT, LANES - COARSE_AT - CLUSTERS * MODES))
    )
    inverse, multipliers, projected, values, *sent = call(
        first_kernel,
        (shape(LANES, LANES), VECTOR, VECTOR, VECTOR, *SENT),
        [SMEM] + [VMEM] * 9,
        [PICKS], 1 << 30, SMALL, "first",
    )(where, table, *sums, spread_load, modes, dual, paired)
    sums, image = meet(values, sent)
    before, moved, newer, values, *sent = call(
        second_kernel,
        (shape(LOADS, LANES), VECTOR, VECTOR, VECTOR, *SENT),
        [SMEM] + [VMEM] * 11,
        [PICKS], 1 << 30, SMALL, "second",
    )(where, table, *sums, inverse, modes, dual, image, multipliers, projected)
    sums, paired = meet(values, sent)
    multipliers, projected = call(
        last_kernel,
        (VECTOR, VECTOR),
        [VMEM] * 13,
        [], 1 << 30, SMALL, "last",
    )(*sums, before, inverse, modes, paired, image, moved, projected, newer, ranks)
    return (multipliers.T[None], projected.T[None])


def solution(mesh):
    return jax.shard_map(
        local,
        mesh=mesh,
        in_specs=(
            P(("cluster", "sub"), None, None, None),
            P(("cluster", "sub"), None, None),
            P(("cluster", "sub"), None, None),
            P(),
            P(("cluster", "sub"), None, None),
            P(("cluster", "sub"), None),
        ),
        out_specs=(P(("cluster", "sub"), None, None), P(("cluster", "sub"), None, None)),
        check_vma=False,
    )
```

profile of v0, /device:TPU:1, one launch (start us, length us, event | category | flops | bytes accessed | tf_op | source)
XLA Modules:
  0.0 159.2 jit_solution(3015585858663436083)
XLA Ops:
  3.1 6.1 %prepare.1 = (s32[8,1152]{1,0:T(8,128)S(1)}, s32[640,1]{1,0:T(8,128)S(1)}, f32[640,1]{1,0:T(8,128)S(1)}, s32[1,640]{1,0:T(1,128)S(1)}, s32[16]{0:T(128)S(1)}, /*...) custom-call(s32[2]{0:T(128)S(1)} %pad_add_fusion.where, ...), custom_call_target="tpu_custom_call" | custom-call | flops 1073741824 | bytes 4194304 | tf_op jit(solution)/shard_map/prepare/pallas_call | solution.py:649
  9.2 4.0 %collective-permute-start = (f32[8,128]{1,0:T(8,128)S(1)}, f32[8,128]{1,0:T(8,128)S(1)}, u32[]{:S(2)}, u32[]{:S(2)}) collective-permute-start(f32[8,128]{1,0:T(8,128)S(1)} %get-tuple-element.37), channel_id=1, source_target_pairs={{0,32},{32,64},{64,96},{1,33},{33,65},{65,97},{2,34},{34,66},{66,9... | collective-permute-start | bytes 12296 | tf_op jit(solution)/shard_map/ppermute | solution.py:629
  14.5 8.9 %all-to-all-start = ((f32[32,8,128]{2,1,0:T(8,128)}), f32[32,8,128]{2,1,0:T(8,128)S(1)}, u32[]{:S(2)}, u32[]{:S(2)}) async-start(f32[32,8,128]{2,1,0:T(8,128)} %get-tuple-element.36), calls=%async_computation | async-start | bytes 262144 | tf_op jit(solution)/shard_map/all_to_all | solution.py:631
  24.4 39.7 %solve.1 = (f32[640,640]{1,0:T(8,128)S(1)}, f32[32,640]{1,0:T(8,128)S(1)}) custom-call(s32[16]{0:T(128)S(1)} %get-tuple-element.39.counts, f32[300,128,128]{2,1,0:T(8,128)} %bitcast.19, s32[640,1]{1,0:T(8,128)S(1)} %get-tuple-element.40.unknown, f32[640,1]{1,0:T(8,128)S(1)} %get-tuple-element.41.signs, f32[32,3072]{1,0:T(8,128)S(1)} %bitcast.15), custom_call_target="tpu_custom_call" | custom-call | flops 32212254720 | bytes 20971520 | tf_op jit(solution)/shard_map/solve/pallas_call | solution.py:604
  64.2 4.8 %start.1 = (f32[128,640]{1,0:T(8,128)S(1)}, f32[56,640]{1,0:T(8,128)S(1)}, f32[32,56,128]{2,1,0:T(8,128)}, f32[56,128]{1,0:T(8,128)S(1)}, f32[56,128]{1,0:T(8,128)S(1)}) custom-call(s32[2]{0:T(128)S(1)} %pad_add_fusion.where, s32[8,1152]{1,0:T(8,128)S(1)} %get-tuple-element.34.table, f32[8,640]{1,0:T(8,128)S(1)} %get-tuple-element.35.half, ...), custom_call_target="tpu_custom_call" | custom-call | flops 1073741824 | bytes 4194304 | tf_op jit(solution)/shard_map/start/pallas_call | solution.py:668
  69.0 9.0 %all-to-all-start.1 = ((f32[32,56,128]{2,1,0:T(8,128)}), f32[32,56,128]{2,1,0:T(8,128)S(1)}, u32[]{:S(2)}, u32[]{:S(2)}) async-start(f32[32,56,128]{2,1,0:T(8,128)} %get-tuple-element.44), calls=%async_computation.1 | async-start | bytes 1835008 | tf_op jit(solution)/shard_map/all_to_all | solution.py:631
  78.0 5.1 %collective-permute-start.5 = (f32[56,128]{1,0:T(8,128)S(1)}, f32[56,128]{1,0:T(8,128)S(1)}, u32[]{:S(2)}, u32[]{:S(2)}) collective-permute-start(f32[56,128]{1,0:T(8,128)S(1)} %get-tuple-element.47), channel_id=1, source_target_pairs={{0,32},{32,64},{64,96},{1,33},{33,65},{65,97},{2,34},{34,66},{66,9... | collective-permute-start | bytes 86024 | tf_op jit(solution)/shard_map/ppermute | solution.py:629
  84.6 9.0 %all-to-all-done.1.sub = f32[32,56,128]{2,1,0:T(8,128)S(1)} async-done(((f32[32,56,128]{2,1,0:T(8,128)}), f32[32,56,128]{2,1,0:T(8,128)S(1)}, u32[]{:S(2)}, u32[]{:S(2)}) %all-to-all-start.1) | async-done | bytes 917536 | tf_op jit(solution)/shard_map/all_to_all | solution.py:631
  93.6 3.3 %collective-permute-start.2 = (f32[56,128]{1,0:T(8,128)S(1)}, f32[56,128]{1,0:T(8,128)S(1)}, u32[]{:S(2)}, u32[]{:S(2)}) collective-permute-start(f32[56,128]{1,0:T(8,128)S(1)} %reduce_sum.27.s0), channel_id=1, source_target_pairs={{0,32},{32,64},{64,96},{96,0},{1,33},{33,65},{65,97},{97,1},{2,34}... | collective-permute-start | bytes 86024 | tf_op jit(solution)/shard_map/ppermute | solution.py:638
  96.9 1.6 %collective-permute-start.3 = (f32[56,128]{1,0:T(8,128)S(1)}, f32[56,128]{1,0:T(8,128)S(1)}, u32[]{:S(2)}, u32[]{:S(2)}) collective-permute-start(f32[56,128]{1,0:T(8,128)S(1)} %reduce_sum.27.s0), channel_id=1, source_target_pairs={{0,64},{32,96},{64,0},{96,32},{1,65},{33,97},{65,1},{97,33},{2,66}... | collective-permute-start | bytes 86024 | tf_op jit(solution)/shard_map/ppermute | solution.py:638
  99.9 1.6 %pair.3.paired = f32[56,640]{1,0:T(8,128)S(1)} custom-call(s32[2]{0:T(128)S(1)} %pad_add_fusion.where, s32[8,1152]{1,0:T(8,128)S(1)} %get-tuple-element.34.table, f32[56,640]{1,0:T(8,128)S(1)} %get-tuple-element.46.values, f32[32,56,128]{2,1,0:T(8,128)S(1)} %all-to-all-done.1.sub, f32[56,128]{1,0:T(8,128)S(1)} %collective-permute-done.5.lower, ...), custom_call_target="tpu_custom_call" | custom-call | flops 1073741824 | bytes 4194304 | tf_op jit(solution)/shard_map/pair/pallas_call | solution.py:678
  101.6 7.1 %first.1 = (f32[128,128]{1,0:T(8,128)S(1)}, f32[32,640]{1,0:T(8,128)S(1)}, f32[32,640]{1,0:T(8,128)S(1)}, f32[32,640]{1,0:T(8,128)S(1)}, f32[32,32,128]{2,1,0:T(...) custom-call(s32[2]{0:T(128)S(1)} %pad_add_fusion.where, s32[8,1152]{1,0:T(8,128)S(1)} %get-tuple-element.34.table, ...), custom_call_target="tpu_custom_call" | custom-call | flops 1073741824 | bytes 4194304 | tf_op jit(solution)/shard_map/first/pallas_call | solution.py:690
  108.6 5.3 %all-to-all-start.2 = ((f32[32,32,128]{2,1,0:T(8,128)}), f32[32,32,128]{2,1,0:T(8,128)S(1)}, u32[]{:S(2)}, u32[]{:S(2)}) async-start(f32[32,32,128]{2,1,0:T(8,128)} %get-tuple-element.49), calls=%async_computation.2 | async-start | bytes 1048576 | tf_op jit(solution)/shard_map/all_to_all | solution.py:631
  113.9 2.1 %collective-permute-start.10 = (f32[32,128]{1,0:T(8,128)S(1)}, f32[32,128]{1,0:T(8,128)S(1)}, u32[]{:S(2)}, u32[]{:S(2)}) collective-permute-start(f32[32,128]{1,0:T(8,128)S(1)} %get-tuple-element.52), channel_id=1, source_target_pairs={{0,32},{32,64},{64,96},{1,33},{33,65},{65,97},{2,34},{34,66},{66,9... | collective-permute-start | bytes 49160 | tf_op jit(solution)/shard_map/ppermute | solution.py:629
  117.3 8.2 %all-to-all-done.2.sub = f32[32,32,128]{2,1,0:T(8,128)S(1)} async-done(((f32[32,32,128]{2,1,0:T(8,128)}), f32[32,32,128]{2,1,0:T(8,128)S(1)}, u32[]{:S(2)}, u32[]{:S(2)}) %all-to-all-start.2) | async-done | bytes 524320 | tf_op jit(solution)/shard_map/all_to_all | solution.py:631
  125.8 3.6 %collective-permute-start.8 = (f32[32,128]{1,0:T(8,128)S(1)}, f32[32,128]{1,0:T(8,128)S(1)}, u32[]{:S(2)}, u32[]{:S(2)}) collective-permute-start(f32[32,128]{1,0:T(8,128)S(1)} %reduce_sum.28.s0), channel_id=1, source_target_pairs={{0,64},{32,96},{64,0},{96,32},{1,65},{33,97},{65,1},{97,33},{2,66}... | collective-permute-start | bytes 49160 | tf_op jit(solution)/shard_map/ppermute | solution.py:638
  129.4 1.6 pair.4.image
  132.0 3.8 %second.1 = (f32[32,128]{1,0:T(8,128)S(1)}, f32[32,640]{1,0:T(8,128)S(1)}, f32[32,640]{1,0:T(8,128)S(1)}, f32[32,640]{1,0:T(8,128)S(1)}, f32[32,32,128]{2,1,0:T(...) custom-call(s32[2]{0:T(128)S(1)} %pad_add_fusion.where, s32[8,1152]{1,0:T(8,128)S(1)} %get-tuple-element.34.table, ...), custom_call_target="tpu_custom_call" | custom-call | flops 1073741824 | bytes 4194304 | tf_op jit(solution)/shard_map/second/pallas_call | solution.py:697
  135.7 5.3 %all-to-all-start.3 = ((f32[32,32,128]{2,1,0:T(8,128)}), f32[32,32,128]{2,1,0:T(8,128)S(1)}, u32[]{:S(2)}, u32[]{:S(2)}) async-start(f32[32,32,128]{2,1,0:T(8,128)} %get-tuple-element.56), calls=%async_computation.3 | async-start | bytes 1048576 | tf_op jit(solution)/shard_map/all_to_all | solution.py:631
  141.1 1.5 collective-permute-start.15
  143.9 8.8 %all-to-all-done.3.sub = f32[32,32,128]{2,1,0:T(8,128)S(1)} async-done(((f32[32,32,128]{2,1,0:T(8,128)}), f32[32,32,128]{2,1,0:T(8,128)S(1)}, u32[]{:S(2)}, u32[]{:S(2)}) %all-to-all-start.3) | async-done | bytes 524320 | tf_op jit(solution)/shard_map/all_to_all | solution.py:631
  152.8 2.1 %collective-permute-start.13 = (f32[32,128]{1,0:T(8,128)S(1)}, f32[32,128]{1,0:T(8,128)S(1)}, u32[]{:S(2)}, u32[]{:S(2)}) collective-permute-start(f32[32,128]{1,0:T(8,128)S(1)} %reduce_sum.29.s0), channel_id=1, source_target_pairs={{0,64},{32,96},{64,0},{96,32},{1,65},{33,97},{65,1},{97,33},{2,66}... | collective-permute-start | bytes 49160 | tf_op jit(solution)/shard_map/ppermute | solution.py:638
  156.1 1.6 pair.5.paired
  157.7 1.6 last.1
  (43 shorter events, 12.8 us)
Async XLA Ops:
  0.7 0.9 copy-start.1
  9.2 55.0 %collective-permute-start = (f32[8,128]{1,0:T(8,128)S(1)}, f32[8,128]{1,0:T(8,128)S(1)}, u32[]{:S(2)}, u32[]{:S(2)}) collective-permute-start(f32[8,128]{1,0:T(8,128)S(1)} %get-tuple-element.37), channel_id=1, source_target_pairs={{0,32},{32,64},{64,96},{1,33},{33,65},{65,97},{2,34},{34,66},{66,9... | collective-permute-start | bytes 12296 | tf_op jit(solution)/shard_map/ppermute | solution.py:629
  13.2 51.0 %collective-permute-start.1 = (f32[8,128]{1,0:T(8,128)S(1)}, f32[8,128]{1,0:T(8,128)S(1)}, u32[]{:S(2)}, u32[]{:S(2)}) collective-permute-start(f32[8,128]{1,0:T(8,128)S(1)} %get-tuple-element.38), channel_id=1, source_target_pairs={{32,0},{64,32},{96,64},{33,1},{65,33},{97,65},{34,2},{66,34},{98,6... | collective-permute-start | bytes 12296 | tf_op jit(solution)/shard_map/ppermute | solution.py:630
  14.5 49.7 %all-to-all-start = ((f32[32,8,128]{2,1,0:T(8,128)}), f32[32,8,128]{2,1,0:T(8,128)S(1)}, u32[]{:S(2)}, u32[]{:S(2)}) async-start(f32[32,8,128]{2,1,0:T(8,128)} %get-tuple-element.36), calls=%async_computation | async-start | bytes 262144 | tf_op jit(solution)/shard_map/all_to_all | solution.py:631
  23.4 1.0 copy-start
  24.4 60.0 %copy-start.4 = (f32[24,32]{1,0:T(8,128)S(1)}, f32[24,32]{1,0:T(8,128)}, u32[]{:S(2)}) copy-start(f32[24,32]{1,0:T(8,128)} %param.9) | copy-start | bytes 9220
  69.0 24.6 %all-to-all-start.1 = ((f32[32,56,128]{2,1,0:T(8,128)}), f32[32,56,128]{2,1,0:T(8,128)S(1)}, u32[]{:S(2)}, u32[]{:S(2)}) async-start(f32[32,56,128]{2,1,0:T(8,128)} %get-tuple-element.44), calls=%async_computation.1 | async-start | bytes 1835008 | tf_op jit(solution)/shard_map/all_to_all | solution.py:631
  78.0 21.8 %collective-permute-start.5 = (f32[56,128]{1,0:T(8,128)S(1)}, f32[56,128]{1,0:T(8,128)S(1)}, u32[]{:S(2)}, u32[]{:S(2)}) collective-permute-start(f32[56,128]{1,0:T(8,128)S(1)} %get-tuple-element.47), channel_id=1, source_target_pairs={{0,32},{32,64},{64,96},{1,33},{33,65},{65,97},{2,34},{34,66},{66,9... | collective-permute-start | bytes 86024 | tf_op jit(solution)/shard_map/ppermute | solution.py:629
  83.1 16.7 %collective-permute-start.6 = (f32[56,128]{1,0:T(8,128)S(1)}, f32[56,128]{1,0:T(8,128)S(1)}, u32[]{:S(2)}, u32[]{:S(2)}) collective-permute-start(f32[56,128]{1,0:T(8,128)S(1)} %get-tuple-element.48), channel_id=1, source_target_pairs={{32,0},{64,32},{96,64},{33,1},{65,33},{97,65},{34,2},{66,34},{98,6... | collective-permute-start | bytes 86024 | tf_op jit(solution)/shard_map/ppermute | solution.py:630
  93.6 7.9 %collective-permute-start.2 = (f32[56,128]{1,0:T(8,128)S(1)}, f32[56,128]{1,0:T(8,128)S(1)}, u32[]{:S(2)}, u32[]{:S(2)}) collective-permute-start(f32[56,128]{1,0:T(8,128)S(1)} %reduce_sum.27.s0), channel_id=1, source_target_pairs={{0,32},{32,64},{64,96},{96,0},{1,33},{33,65},{65,97},{97,1},{2,34}... | collective-permute-start | bytes 86024 | tf_op jit(solution)/shard_map/ppermute | solution.py:638
  96.9 4.6 %collective-permute-start.3 = (f32[56,128]{1,0:T(8,128)S(1)}, f32[56,128]{1,0:T(8,128)S(1)}, u32[]{:S(2)}, u32[]{:S(2)}) collective-permute-start(f32[56,128]{1,0:T(8,128)S(1)} %reduce_sum.27.s0), channel_id=1, source_target_pairs={{0,64},{32,96},{64,0},{96,32},{1,65},{33,97},{65,1},{97,33},{2,66}... | collective-permute-start | bytes 86024 | tf_op jit(solution)/shard_map/ppermute | solution.py:638
  98.5 3.0 %collective-permute-start.4 = (f32[56,128]{1,0:T(8,128)S(1)}, f32[56,128]{1,0:T(8,128)S(1)}, u32[]{:S(2)}, u32[]{:S(2)}) collective-permute-start(f32[56,128]{1,0:T(8,128)S(1)} %reduce_sum.27.s0), channel_id=1, source_target_pairs={{0,96},{32,0},{64,32},{96,64},{1,97},{33,1},{65,33},{97,65},{2,98}... | collective-permute-start | bytes 86024 | tf_op jit(solution)/shard_map/ppermute | solution.py:638
  108.6 16.9 %all-to-all-start.2 = ((f32[32,32,128]{2,1,0:T(8,128)}), f32[32,32,128]{2,1,0:T(8,128)S(1)}, u32[]{:S(2)}, u32[]{:S(2)}) async-start(f32[32,32,128]{2,1,0:T(8,128)} %get-tuple-element.49), calls=%async_computation.2 | async-start | bytes 1048576 | tf_op jit(solution)/shard_map/all_to_all | solution.py:631
  113.9 15.4 %collective-permute-start.10 = (f32[32,128]{1,0:T(8,128)S(1)}, f32[32,128]{1,0:T(8,128)S(1)}, u32[]{:S(2)}, u32[]{:S(2)}) collective-permute-start(f32[32,128]{1,0:T(8,128)S(1)} %get-tuple-element.52), channel_id=1, source_target_pairs={{0,32},{32,64},{64,96},{1,33},{33,65},{65,97},{2,34},{34,66},{66,9... | collective-permute-start | bytes 49160 | tf_op jit(solution)/shard_map/ppermute | solution.py:629
  116.0 13.4 %collective-permute-start.11 = (f32[32,128]{1,0:T(8,128)S(1)}, f32[32,128]{1,0:T(8,128)S(1)}, u32[]{:S(2)}, u32[]{:S(2)}) collective-permute-start(f32[32,128]{1,0:T(8,128)S(1)} %get-tuple-element.53), channel_id=1, source_target_pairs={{32,0},{64,32},{96,64},{33,1},{65,33},{97,65},{34,2},{66,34},{98,6... | collective-permute-start | bytes 49160 | tf_op jit(solution)/shard_map/ppermute | solution.py:630
  125.6 5.4 %collective-permute-start.7 = (f32[32,128]{1,0:T(8,128)S(1)}, f32[32,128]{1,0:T(8,128)S(1)}, u32[]{:S(2)}, u32[]{:S(2)}) collective-permute-start(f32[32,128]{1,0:T(8,128)S(1)} %reduce_sum.28.s0), channel_id=1, source_target_pairs={{0,32},{32,64},{64,96},{96,0},{1,33},{33,65},{65,97},{97,1},{2,34}... | collective-permute-start | bytes 49160 | tf_op jit(solution)/shard_map/ppermute | solution.py:638
  125.8 5.2 %collective-permute-start.8 = (f32[32,128]{1,0:T(8,128)S(1)}, f32[32,128]{1,0:T(8,128)S(1)}, u32[]{:S(2)}, u32[]{:S(2)}) collective-permute-start(f32[32,128]{1,0:T(8,128)S(1)} %reduce_sum.28.s0), channel_id=1, source_target_pairs={{0,64},{32,96},{64,0},{96,32},{1,65},{33,97},{65,1},{97,33},{2,66}... | collective-permute-start | bytes 49160 | tf_op jit(solution)/shard_map/ppermute | solution.py:638
  129.4 2.6 %collective-permute-start.9 = (f32[32,128]{1,0:T(8,128)S(1)}, f32[32,128]{1,0:T(8,128)S(1)}, u32[]{:S(2)}, u32[]{:S(2)}) collective-permute-start(f32[32,128]{1,0:T(8,128)S(1)} %reduce_sum.28.s0), channel_id=1, source_target_pairs={{0,96},{32,0},{64,32},{96,64},{1,97},{33,1},{65,33},{97,65},{2,98}... | collective-permute-start | bytes 49160 | tf_op jit(solution)/shard_map/ppermute | solution.py:638
  135.7 16.9 %all-to-all-start.3 = ((f32[32,32,128]{2,1,0:T(8,128)}), f32[32,32,128]{2,1,0:T(8,128)S(1)}, u32[]{:S(2)}, u32[]{:S(2)}) async-start(f32[32,32,128]{2,1,0:T(8,128)} %get-tuple-element.56), calls=%async_computation.3 | async-start | bytes 1048576 | tf_op jit(solution)/shard_map/all_to_all | solution.py:631
  141.1 15.0 %collective-permute-start.15 = (f32[32,128]{1,0:T(8,128)S(1)}, f32[32,128]{1,0:T(8,128)S(1)}, u32[]{:S(2)}, u32[]{:S(2)}) collective-permute-start(f32[32,128]{1,0:T(8,128)S(1)} %get-tuple-element.59), channel_id=1, source_target_pairs={{0,32},{32,64},{64,96},{1,33},{33,65},{65,97},{2,34},{34,66},{66,9... | collective-permute-start | bytes 49160 | tf_op jit(solution)/shard_map/ppermute | solution.py:629
  142.6 13.5 %collective-permute-start.16 = (f32[32,128]{1,0:T(8,128)S(1)}, f32[32,128]{1,0:T(8,128)S(1)}, u32[]{:S(2)}, u32[]{:S(2)}) collective-permute-start(f32[32,128]{1,0:T(8,128)S(1)} %get-tuple-element.60), channel_id=1, source_target_pairs={{32,0},{64,32},{96,64},{33,1},{65,33},{97,65},{34,2},{66,34},{98,6... | collective-permute-start | bytes 49160 | tf_op jit(solution)/shard_map/ppermute | solution.py:630
  152.7 4.9 %collective-permute-start.12 = (f32[32,128]{1,0:T(8,128)S(1)}, f32[32,128]{1,0:T(8,128)S(1)}, u32[]{:S(2)}, u32[]{:S(2)}) collective-permute-start(f32[32,128]{1,0:T(8,128)S(1)} %reduce_sum.29.s0), channel_id=1, source_target_pairs={{0,32},{32,64},{64,96},{96,0},{1,33},{33,65},{65,97},{97,1},{2,34}... | collective-permute-start | bytes 49160 | tf_op jit(solution)/shard_map/ppermute | solution.py:638
  152.8 4.9 %collective-permute-start.13 = (f32[32,128]{1,0:T(8,128)S(1)}, f32[32,128]{1,0:T(8,128)S(1)}, u32[]{:S(2)}, u32[]{:S(2)}) collective-permute-start(f32[32,128]{1,0:T(8,128)S(1)} %reduce_sum.29.s0), channel_id=1, source_target_pairs={{0,64},{32,96},{64,0},{96,32},{1,65},{33,97},{65,1},{97,33},{2,66}... | collective-permute-start | bytes 49160 | tf_op jit(solution)/shard_map/ppermute | solution.py:638
  154.9 2.8 %collective-permute-start.14 = (f32[32,128]{1,0:T(8,128)S(1)}, f32[32,128]{1,0:T(8,128)S(1)}, u32[]{:S(2)}, u32[]{:S(2)}) collective-permute-start(f32[32,128]{1,0:T(8,128)S(1)} %reduce_sum.29.s0), channel_id=1, source_target_pairs={{0,96},{32,0},{64,32},{96,64},{1,97},{33,1},{65,33},{97,65},{2,98}... | collective-permute-start | bytes 49160 | tf_op jit(solution)/shard_map/ppermute | solution.py:638
  (2 other events, 1.5 us)
where the time goes:
time: 160 us; the launch traced here: 159 us
  Pallas kernels  67.8 us (42%)
  starting transfers between devices  59.8 us (37%)
  waiting for transfers between devices  27 us (17%)
  local copies, waits for them, and re-layouts  3.51 us (2%)
    pallas_call x1, Pallas kernels, run_solve(): call(solve_kernel, (shape(SLOTS, SLOTS), VECTOR), [SMEM, ANY] + [VMEM] *...  39.7 us
    all_to_all x4, starting transfers between devices, exchange(): lax.all_to_all(to_sub, 'sub', split_axis=0, concat_axis=0, tiled=True)  28.5 us
    all_to_all x4, waiting for transfers between devices, exchange(): lax.all_to_all(to_sub, 'sub', split_axis=0, concat_axis=0, tiled=True)  25.9 us
    ppermute x9, starting transfers between devices, cluster_sums(): lax.ppermute(own, 'cluster', [(c, (c + by) % CLUSTERS) for c in range(CLU...  13.4 us
    ppermute x4, starting transfers between devices, exchange(): from_lower = lax.ppermute(to_upper, 'cluster', up)  12.7 us
    pallas_call x1, Pallas kernels, local(): call(first_kernel, (shape(LANES, LANES), VECTOR, VECTOR, VECTOR, *SENT),...  7.08 us
    pallas_call x1, Pallas kernels, local(): call(prepare_kernel, (shape(8, PLACES * LANES, dtype=jnp.int32), shape(SL...  6.13 us
    ppermute x4, starting transfers between devices, exchange(): from_upper = lax.ppermute(to_lower, 'cluster', down)  5.17 us
  transfers between devices with their start and end apart: 21, of which 5 were waited for; matrix products, arithmetic and copies ran while one was open for 0% of the time, Pallas kernels for 28%

commit v1 on v0

--- a/solution.py
+++ b/solution.py
@@ -39,6 +39,7 @@
 VMEM = pl.BlockSpec(memory_space=pltpu.VMEM)
 SMEM = pl.BlockSpec(memory_space=pltpu.SMEM)
 ANY = pl.BlockSpec(memory_space=pl.ANY)
+HBM = pl.BlockSpec(memory_space=pltpu.HBM)
 
 
 def nt(a, b, precision=None):
@@ -170,11 +171,20 @@
 
 
 def prepare_kernel(
-    where, peer_slots, unknown_row, rigid,
+    where, peer_slots_hbm, unknown_hbm, rigid_hbm,
     table, sorted_unknown, signs, ranks, counts, half, to_sub, to_lower, to_upper,
-    peer_table, picks,
+    peer_table, picks, peer_slots, unknown_row, rigid, sems,
 ):
     me, cluster = where[0], where[1]
+    copies = [
+        pltpu.make_async_copy(peer_slots_hbm, peer_slots, sems.at[0]),
+        pltpu.make_async_copy(unknown_hbm, unknown_row, sems.at[1]),
+        pltpu.make_async_copy(rigid_hbm, rigid, sems.at[2]),
+    ]
+    for copy in copies:
+        copy.start()
+    for copy in copies:
+        copy.wait()
     devices = peer_slots.shape[1]
     listed = jnp.concatenate(
         [
@@ -250,7 +260,7 @@
 
 
 def invert_diagonal(diag, beside, inverse, high, low):
-    base, group, some, many = 32, 8, 12, 12
+    base, group, some, many = 32, 8, 12, 24
     lane3 = lax.broadcasted_iota(jnp.int32, (some, group, TILE), 2)
     row = lax.broadcasted_iota(jnp.int32, (some, group, TILE), 1)
     flat_lane = lax.broadcasted_iota(jnp.int32, (some * group, TILE), 1)
@@ -337,14 +347,14 @@
 
 
 def solve_kernel(
-    counts, tiles, unknown, signs, loads, dual, load,
-    held, xh, xl, total, diag, beside, inverse, high, low, sems, early_sems,
+    counts, tiles, unknown, signs, loads_hbm, dual, load,
+    loads, held, xh, xl, total, diag, beside, inverse, high, low, sems, early_sems, load_sem,
 ):
     def copy(c):
         at = pl.ds(c * CHUNK, CHUNK)
         return pltpu.make_async_copy(tiles.at[at], held.at[at], sems.at[c])
 
-    early = []
+    early = [pltpu.make_async_copy(loads_hbm, loads, load_sem.at[0])]
     for t in range(TILE_ROWS):
         at = t * (t + 1) // 2 + t
         early.append(pltpu.make_async_copy(tiles.at[at], diag.at[t], early_sems.at[t]))
@@ -360,12 +370,12 @@
         copy(c).start()
     dual[...] = jnp.zeros_like(dual)
     load[...] = jnp.zeros_like(load)
+    for one in early:
+        one.wait()
     lane = lax.broadcasted_iota(jnp.int32, (SLOTS, BLOCK), 1)
     for i in range(BLOCKS):
         total[i, :LOADS] = loads[:, i * BLOCK : (i + 1) * BLOCK]
         total[i, LOADS:] = jnp.where(unknown[...] - i * BLOCK == lane, signs[...], 0.0)
-    for one in early:
-        one.wait()
     invert_diagonal(diag, beside, inverse, high, low)
     for c in range(CHUNKS):
         copy(c).wait()
@@ -604,8 +614,9 @@
     return call(
         solve_kernel,
         (shape(SLOTS, SLOTS), VECTOR),
-        [SMEM, ANY] + [VMEM] * 3,
+        [SMEM, ANY, VMEM, VMEM, HBM],
         [
+            pltpu.VMEM((LOADS, UNKNOWNS), F32),
             pltpu.VMEM(tiles.shape, F32),
             pltpu.VMEM((RHS, BLOCK), BF16),
             pltpu.VMEM((RHS, BLOCK), BF16),
@@ -617,6 +628,7 @@
             pltpu.VMEM((BLOCKS, BLOCK, BLOCK), BF16),
             pltpu.SemaphoreType.DMA((CHUNKS,)),
             pltpu.SemaphoreType.DMA((TILE_ROWS + BLOCKS,)),
+            pltpu.SemaphoreType.DMA((1,)),
         ],
         30 << 30, 5 * SMALL, "solve", 50,
     )(counts, tiles, unknown, signs, loads)
@@ -657,9 +669,16 @@
             shape(8, SLOTS),
             *sent_shapes(8),
         ),
-        [SMEM, VMEM, VMEM, VMEM],
-        [pltpu.VMEM((CLUSTERS * SUBS, LANES), jnp.int32), PICKS],
-        1 << 30, SMALL, "prepare",
+        [SMEM, HBM, HBM, HBM],
+        [
+            pltpu.VMEM((CLUSTERS * SUBS, LANES), jnp.int32),
+            PICKS,
+            pltpu.VMEM(peer_slots.shape[:0:-1], jnp.int32),
+            pltpu.VMEM(slot_unknown.shape, jnp.int32),
+            pltpu.VMEM((MODES, 1, UNKNOWNS), F32),
+            pltpu.SemaphoreType.DMA((3,)),
+        ],
+        1 << 30, SMALL, "prepare", 60,
         out_specs=(VMEM, VMEM, VMEM, VMEM, SMEM, VMEM, VMEM, VMEM, VMEM),
     )(where, peer_slots[0].T, slot_unknown, jnp.swapaxes(rigid_modes, 0, 1))
     received = exchange(sent)

time: 160 us -> 162 us (1.012)
  Pallas kernels: 67.8 us -> 70.1 us
  starting transfers between devices: 59.8 us -> 58 us
    unnamed x11 -> x19, local copies, waits for them, and re-layouts: 3.43 us -> 3.64 us
  transfers between devices with their start and end apart: 21 -> 21, of which waited for: 5 -> 4; matrix products, arithmetic and copies ran while one was open for 0% -> 0% of each run, Pallas kernels for 28% -> 28%
where the time goes in v1:
time: 162 us; the launch traced here: 161 us
  Pallas kernels  70.1 us (43%)
  starting transfers between devices  58 us (36%)
  waiting for transfers between devices  27.5 us (17%)
  local copies, waits for them, and re-layouts  3.71 us (2%)
    pallas_call x1, Pallas kernels, run_solve(): call(solve_kernel, (shape(SLOTS, SLOTS), VECTOR), [SMEM, ANY, VMEM, VMEM,...  40.7 us
    all_to_all x4, starting transfers between devices, exchange(): lax.all_to_all(to_sub, 'sub', split_axis=0, concat_axis=0, tiled=True)  27.1 us
    all_to_all x4, waiting for transfers between devices, exchange(): lax.all_to_all(to_sub, 'sub', split_axis=0, concat_axis=0, tiled=True)  26.5 us
    ppermute x9, starting transfers between devices, cluster_sums(): lax.ppermute(own, 'cluster', [(c, (c + by) % CLUSTERS) for c in range(CLU...  13.6 us
    ppermute x4, starting transfers between devices, exchange(): from_lower = lax.ppermute(to_upper, 'cluster', up)  12.2 us
    pallas_call x1, Pallas kernels, local(): call(prepare_kernel, (shape(8, PLACES * LANES, dtype=jnp.int32), shape(SL...  7.47 us
    pallas_call x1, Pallas kernels, local(): call(first_kernel, (shape(LANES, LANES), VECTOR, VECTOR, VECTOR, *SENT),...  7.12 us
    ppermute x4, starting transfers between devices, exchange(): from_upper = lax.ppermute(to_lower, 'cluster', down)  5.17 us
  transfers between devices with their start and end apart: 21, of which 4 were waited for; matrix products, arithmetic and copies ran while one was open for 0% of the time, Pallas kernels for 28%

profile of v1, /device:TPU:1, one launch (start us, length us, event | category | flops | bytes accessed | tf_op | source)
XLA Modules:
  0.0 161.1 jit_solution(69986721078191492)
XLA Ops:
  1.3 7.5 %prepare.1 = (s32[8,1152]{1,0:T(8,128)}, s32[640,1]{1,0:T(8,128)}, f32[640,1]{1,0:T(8,128)}, s32[1,640]{1,0:T(1,128)}, s32[16]{0:T(128)}, /*index=5*/f32[8,640]{...) custom-call(s32[2]{0:T(128)} %pad_add_fusion.where, s32[96,128]{1,0:T(8,128)} %bitcast.19, ...), custom_call_target="tpu_custom_call" | custom-call | flops 1073741824 | bytes 4194304 | tf_op jit(solution)/shard_map/prepare/pallas_call | solution.py:661
  8.8 4.0 %collective-permute-start = (f32[8,128]{1,0:T(8,128)}, f32[8,128]{1,0:T(8,128)S(1)}, u32[]{:S(2)}, u32[]{:S(2)}) collective-permute-start(f32[8,128]{1,0:T(8,128)} %get-tuple-element.37), channel_id=1, source_target_pairs={{0,32},{32,64},{64,96},{1,33},{33,65},{65,97},{2,34},{34,66},{66,9... | collective-permute-start | bytes 12296 | tf_op jit(solution)/shard_map/ppermute | solution.py:641
  14.1 8.9 %all-to-all-start = ((f32[32,8,128]{2,1,0:T(8,128)}), f32[32,8,128]{2,1,0:T(8,128)S(1)}, u32[]{:S(2)}, u32[]{:S(2)}) async-start(f32[32,8,128]{2,1,0:T(8,128)} %get-tuple-element.36), calls=%async_computation | async-start | bytes 262144 | tf_op jit(solution)/shard_map/all_to_all | solution.py:643
  26.6 40.7 %solve.1 = (f32[640,640]{1,0:T(8,128)S(1)}, f32[32,640]{1,0:T(8,128)S(1)}) custom-call(s32[16]{0:T(128)S(1)} %copy-done.7, f32[300,128,128]{2,1,0:T(8,128)} %bitcast.17, s32[640,1]{1,0:T(8,128)S(1)} %copy-done.2, f32[640,1]{1,0:T(8,128)S(1)} %copy-done.3, f32[32,3072]{1,0:T(8,128)S(1)} %bitcast.15), custom_call_target="tpu_custom_call" | custom-call | flops 32212254720 | bytes 20971520 | tf_op jit(solution)/shard_map/solve/pallas_call | solution.py:614
  67.3 4.6 %start.1 = (f32[128,640]{1,0:T(8,128)S(1)}, f32[56,640]{1,0:T(8,128)S(1)}, f32[32,56,128]{2,1,0:T(8,128)}, f32[56,128]{1,0:T(8,128)S(1)}, f32[56,128]{1,0:T(8,128)S(1)}) custom-call(s32[2]{0:T(128)S(1)} %copy-done.1, s32[8,1152]{1,0:T(8,128)S(1)} %copy-done.4, f32[8,640]{1,0:T(8,128)S(1)} %copy-done.5, f32[32,8,128]{2,1,0:T(8,128)S(1)} %all-to-all-done.sub, ...), custom_call_target="tpu_custom_call" | custom-call | flops 1073741824 | bytes 4194304 | tf_op jit(solution)/shard_map/start/pallas_call | solution.py:687
  71.9 8.1 %all-to-all-start.1 = ((f32[32,56,128]{2,1,0:T(8,128)}), f32[32,56,128]{2,1,0:T(8,128)S(1)}, u32[]{:S(2)}, u32[]{:S(2)}) async-start(f32[32,56,128]{2,1,0:T(8,128)} %get-tuple-element.44), calls=%async_computation.1 | async-start | bytes 1835008 | tf_op jit(solution)/shard_map/all_to_all | solution.py:643
  80.0 4.2 %collective-permute-start.5 = (f32[56,128]{1,0:T(8,128)S(1)}, f32[56,128]{1,0:T(8,128)S(1)}, u32[]{:S(2)}, u32[]{:S(2)}) collective-permute-start(f32[56,128]{1,0:T(8,128)S(1)} %get-tuple-element.47), channel_id=1, source_target_pairs={{0,32},{32,64},{64,96},{1,33},{33,65},{65,97},{2,34},{34,66},{66,9... | collective-permute-start | bytes 86024 | tf_op jit(solution)/shard_map/ppermute | solution.py:641
  85.7 9.9 %all-to-all-done.1.sub = f32[32,56,128]{2,1,0:T(8,128)S(1)} async-done(((f32[32,56,128]{2,1,0:T(8,128)}), f32[32,56,128]{2,1,0:T(8,128)S(1)}, u32[]{:S(2)}, u32[]{:S(2)}) %all-to-all-start.1) | async-done | bytes 917536 | tf_op jit(solution)/shard_map/all_to_all | solution.py:643
  95.6 2.3 %collective-permute-start.2 = (f32[56,128]{1,0:T(8,128)S(1)}, f32[56,128]{1,0:T(8,128)S(1)}, u32[]{:S(2)}, u32[]{:S(2)}) collective-permute-start(f32[56,128]{1,0:T(8,128)S(1)} %reduce_sum.27.s0), channel_id=1, source_target_pairs={{0,32},{32,64},{64,96},{96,0},{1,33},{33,65},{65,97},{97,1},{2,34}... | collective-permute-start | bytes 86024 | tf_op jit(solution)/shard_map/ppermute | solution.py:650
  98.0 1.8 %collective-permute-start.3 = (f32[56,128]{1,0:T(8,128)S(1)}, f32[56,128]{1,0:T(8,128)S(1)}, u32[]{:S(2)}, u32[]{:S(2)}) collective-permute-start(f32[56,128]{1,0:T(8,128)S(1)} %reduce_sum.27.s0), channel_id=1, source_target_pairs={{0,64},{32,96},{64,0},{96,32},{1,65},{33,97},{65,1},{97,33},{2,66}... | collective-permute-start | bytes 86024 | tf_op jit(solution)/shard_map/ppermute | solution.py:650
  99.8 1.9 %collective-permute-start.4 = (f32[56,128]{1,0:T(8,128)S(1)}, f32[56,128]{1,0:T(8,128)S(1)}, u32[]{:S(2)}, u32[]{:S(2)}) collective-permute-start(f32[56,128]{1,0:T(8,128)S(1)} %reduce_sum.27.s0), channel_id=1, source_target_pairs={{0,96},{32,0},{64,32},{96,64},{1,97},{33,1},{65,33},{97,65},{2,98}... | collective-permute-start | bytes 86024 | tf_op jit(solution)/shard_map/ppermute | solution.py:650
  101.7 1.8 %pair.3.paired = f32[56,640]{1,0:T(8,128)S(1)} custom-call(s32[2]{0:T(128)S(1)} %copy-done.1, s32[8,1152]{1,0:T(8,128)S(1)} %copy-done.4, f32[56,640]{1,0:T(8,128)S(1)} %get-tuple-element.46.values, f32[32,56,128]{2,1,0:T(8,128)S(1)} %all-to-all-done.1.sub, f32[56,128]{1,0:T(8,128)S(1)} %collective-permute-done.5.lower, ...), custom_call_target="tpu_custom_call" | custom-call | flops 1073741824 | bytes 4194304 | tf_op jit(solution)/shard_map/pair/pallas_call | solution.py:697
  103.5 7.1 %first.1 = (f32[128,128]{1,0:T(8,128)S(1)}, f32[32,640]{1,0:T(8,128)S(1)}, f32[32,640]{1,0:T(8,128)S(1)}, f32[32,640]{1,0:T(8,128)S(1)}, f32[32,32,128]{2,1,0:T(...) custom-call(s32[2]{0:T(128)S(1)} %copy-done.1, s32[8,1152]{1,0:T(8,128)S(1)} %copy-done.4, ...), custom_call_target="tpu_custom_call" | custom-call | flops 1073741824 | bytes 4194304 | tf_op jit(solution)/shard_map/first/pallas_call | solution.py:709
  110.7 4.7 %all-to-all-start.2 = ((f32[32,32,128]{2,1,0:T(8,128)}), f32[32,32,128]{2,1,0:T(8,128)S(1)}, u32[]{:S(2)}, u32[]{:S(2)}) async-start(f32[32,32,128]{2,1,0:T(8,128)} %get-tuple-element.49), calls=%async_computation.2 | async-start | bytes 1048576 | tf_op jit(solution)/shard_map/all_to_all | solution.py:643
  115.4 2.4 %collective-permute-start.10 = (f32[32,128]{1,0:T(8,128)S(1)}, f32[32,128]{1,0:T(8,128)S(1)}, u32[]{:S(2)}, u32[]{:S(2)}) collective-permute-start(f32[32,128]{1,0:T(8,128)S(1)} %get-tuple-element.52), channel_id=1, source_target_pairs={{0,32},{32,64},{64,96},{1,33},{33,65},{65,97},{2,34},{34,66},{66,9... | collective-permute-start | bytes 49160 | tf_op jit(solution)/shard_map/ppermute | solution.py:641
  119.1 7.8 %all-to-all-done.2.sub = f32[32,32,128]{2,1,0:T(8,128)S(1)} async-done(((f32[32,32,128]{2,1,0:T(8,128)}), f32[32,32,128]{2,1,0:T(8,128)S(1)}, u32[]{:S(2)}, u32[]{:S(2)}) %all-to-all-start.2) | async-done | bytes 524320 | tf_op jit(solution)/shard_map/all_to_all | solution.py:643
  127.6 3.6 %collective-permute-start.8 = (f32[32,128]{1,0:T(8,128)S(1)}, f32[32,128]{1,0:T(8,128)S(1)}, u32[]{:S(2)}, u32[]{:S(2)}) collective-permute-start(f32[32,128]{1,0:T(8,128)S(1)} %reduce_sum.28.s0), channel_id=1, source_target_pairs={{0,64},{32,96},{64,0},{96,32},{1,65},{33,97},{65,1},{97,33},{2,66}... | collective-permute-start | bytes 49160 | tf_op jit(solution)/shard_map/ppermute | solution.py:650
  131.2 1.6 pair.4.image
  133.8 3.8 %second.1 = (f32[32,128]{1,0:T(8,128)S(1)}, f32[32,640]{1,0:T(8,128)S(1)}, f32[32,640]{1,0:T(8,128)S(1)}, f32[32,640]{1,0:T(8,128)S(1)}, f32[32,32,128]{2,1,0:T(...) custom-call(s32[2]{0:T(128)S(1)} %copy-done.1, s32[8,1152]{1,0:T(8,128)S(1)} %copy-done.4, ...), custom_call_target="tpu_custom_call" | custom-call | flops 1073741824 | bytes 4194304 | tf_op jit(solution)/shard_map/second/pallas_call | solution.py:716
  137.6 5.3 %all-to-all-start.3 = ((f32[32,32,128]{2,1,0:T(8,128)}), f32[32,32,128]{2,1,0:T(8,128)S(1)}, u32[]{:S(2)}, u32[]{:S(2)}) async-start(f32[32,32,128]{2,1,0:T(8,128)} %get-tuple-element.56), calls=%async_computation.3 | async-start | bytes 1048576 | tf_op jit(solution)/shard_map/all_to_all | solution.py:643
  145.7 8.8 %all-to-all-done.3.sub = f32[32,32,128]{2,1,0:T(8,128)S(1)} async-done(((f32[32,32,128]{2,1,0:T(8,128)}), f32[32,32,128]{2,1,0:T(8,128)S(1)}, u32[]{:S(2)}, u32[]{:S(2)}) %all-to-all-start.3) | async-done | bytes 524320 | tf_op jit(solution)/shard_map/all_to_all | solution.py:643
  154.6 2.1 %collective-permute-start.13 = (f32[32,128]{1,0:T(8,128)S(1)}, f32[32,128]{1,0:T(8,128)S(1)}, u32[]{:S(2)}, u32[]{:S(2)}) collective-permute-start(f32[32,128]{1,0:T(8,128)S(1)} %reduce_sum.29.s0), channel_id=1, source_target_pairs={{0,64},{32,96},{64,0},{96,32},{1,65},{33,97},{65,1},{97,33},{2,66}... | collective-permute-start | bytes 49160 | tf_op jit(solution)/shard_map/ppermute | solution.py:650
  157.9 1.6 pair.5.paired
  159.5 1.5 last.1
  (51 shorter events, 14.1 us)
Async XLA Ops:
  8.8 58.5 %collective-permute-start = (f32[8,128]{1,0:T(8,128)}, f32[8,128]{1,0:T(8,128)S(1)}, u32[]{:S(2)}, u32[]{:S(2)}) collective-permute-start(f32[8,128]{1,0:T(8,128)} %get-tuple-element.37), channel_id=1, source_target_pairs={{0,32},{32,64},{64,96},{1,33},{33,65},{65,97},{2,34},{34,66},{66,9... | collective-permute-start | bytes 12296 | tf_op jit(solution)/shard_map/ppermute | solution.py:641
  12.8 54.4 %collective-permute-start.1 = (f32[8,128]{1,0:T(8,128)}, f32[8,128]{1,0:T(8,128)S(1)}, u32[]{:S(2)}, u32[]{:S(2)}) collective-permute-start(f32[8,128]{1,0:T(8,128)} %get-tuple-element.38), channel_id=1, source_target_pairs={{32,0},{64,32},{96,64},{33,1},{65,33},{97,65},{34,2},{66,34},{98,6... | collective-permute-start | bytes 12296 | tf_op jit(solution)/shard_map/ppermute | solution.py:642
  14.1 53.2 %all-to-all-start = ((f32[32,8,128]{2,1,0:T(8,128)}), f32[32,8,128]{2,1,0:T(8,128)S(1)}, u32[]{:S(2)}, u32[]{:S(2)}) async-start(f32[32,8,128]{2,1,0:T(8,128)} %get-tuple-element.36), calls=%async_computation | async-start | bytes 262144 | tf_op jit(solution)/shard_map/all_to_all | solution.py:643
  26.5 40.7 %copy-start.5 = (f32[8,640]{1,0:T(8,128)S(1)}, f32[8,640]{1,0:T(8,128)}, u32[]{:S(2)}) copy-start(f32[8,640]{1,0:T(8,128)} %get-tuple-element.35.half) | copy-start | bytes 61444
  26.5 59.0 %copy-start.8 = (f32[24,32]{1,0:T(8,128)S(1)}, f32[24,32]{1,0:T(8,128)}, u32[]{:S(2)}) copy-start(f32[24,32]{1,0:T(8,128)} %param.9) | copy-start | bytes 9220
  67.2 92.3 %copy-start.6 = (s32[1,640]{1,0:T(1,128)S(1)}, s32[1,640]{1,0:T(1,128)}, u32[]{:S(2)}) copy-start(s32[1,640]{1,0:T(1,128)} %get-tuple-element.63.ranks) | copy-start | bytes 7684
  71.9 23.7 %all-to-all-start.1 = ((f32[32,56,128]{2,1,0:T(8,128)}), f32[32,56,128]{2,1,0:T(8,128)S(1)}, u32[]{:S(2)}, u32[]{:S(2)}) async-start(f32[32,56,128]{2,1,0:T(8,128)} %get-tuple-element.44), calls=%async_computation.1 | async-start | bytes 1835008 | tf_op jit(solution)/shard_map/all_to_all | solution.py:643
  80.0 21.6 %collective-permute-start.5 = (f32[56,128]{1,0:T(8,128)S(1)}, f32[56,128]{1,0:T(8,128)S(1)}, u32[]{:S(2)}, u32[]{:S(2)}) collective-permute-start(f32[56,128]{1,0:T(8,128)S(1)} %get-tuple-element.47), channel_id=1, source_target_pairs={{0,32},{32,64},{64,96},{1,33},{33,65},{65,97},{2,34},{34,66},{66,9... | collective-permute-start | bytes 86024 | tf_op jit(solution)/shard_map/ppermute | solution.py:641
  84.2 17.5 %collective-permute-start.6 = (f32[56,128]{1,0:T(8,128)S(1)}, f32[56,128]{1,0:T(8,128)S(1)}, u32[]{:S(2)}, u32[]{:S(2)}) collective-permute-start(f32[56,128]{1,0:T(8,128)S(1)} %get-tuple-element.48), channel_id=1, source_target_pairs={{32,0},{64,32},{96,64},{33,1},{65,33},{97,65},{34,2},{66,34},{98,6... | collective-permute-start | bytes 86024 | tf_op jit(solution)/shard_map/ppermute | solution.py:642
  95.6 7.9 %collective-permute-start.2 = (f32[56,128]{1,0:T(8,128)S(1)}, f32[56,128]{1,0:T(8,128)S(1)}, u32[]{:S(2)}, u32[]{:S(2)}) collective-permute-start(f32[56,128]{1,0:T(8,128)S(1)} %reduce_sum.27.s0), channel_id=1, source_target_pairs={{0,32},{32,64},{64,96},{96,0},{1,33},{33,65},{65,97},{97,1},{2,34}... | collective-permute-start | bytes 86024 | tf_op jit(solution)/shard_map/ppermute | solution.py:650
  98.0 5.5 %collective-permute-start.3 = (f32[56,128]{1,0:T(8,128)S(1)}, f32[56,128]{1,0:T(8,128)S(1)}, u32[]{:S(2)}, u32[]{:S(2)}) collective-permute-start(f32[56,128]{1,0:T(8,128)S(1)} %reduce_sum.27.s0), channel_id=1, source_target_pairs={{0,64},{32,96},{64,0},{96,32},{1,65},{33,97},{65,1},{97,33},{2,66}... | collective-permute-start | bytes 86024 | tf_op jit(solution)/shard_map/ppermute | solution.py:650
  99.8 3.8 %collective-permute-start.4 = (f32[56,128]{1,0:T(8,128)S(1)}, f32[56,128]{1,0:T(8,128)S(1)}, u32[]{:S(2)}, u32[]{:S(2)}) collective-permute-start(f32[56,128]{1,0:T(8,128)S(1)} %reduce_sum.27.s0), channel_id=1, source_target_pairs={{0,96},{32,0},{64,32},{96,64},{1,97},{33,1},{65,33},{97,65},{2,98}... | collective-permute-start | bytes 86024 | tf_op jit(solution)/shard_map/ppermute | solution.py:650
  110.7 16.3 %all-to-all-start.2 = ((f32[32,32,128]{2,1,0:T(8,128)}), f32[32,32,128]{2,1,0:T(8,128)S(1)}, u32[]{:S(2)}, u32[]{:S(2)}) async-start(f32[32,32,128]{2,1,0:T(8,128)} %get-tuple-element.49), calls=%async_computation.2 | async-start | bytes 1048576 | tf_op jit(solution)/shard_map/all_to_all | solution.py:643
  115.4 15.8 %collective-permute-start.10 = (f32[32,128]{1,0:T(8,128)S(1)}, f32[32,128]{1,0:T(8,128)S(1)}, u32[]{:S(2)}, u32[]{:S(2)}) collective-permute-start(f32[32,128]{1,0:T(8,128)S(1)} %get-tuple-element.52), channel_id=1, source_target_pairs={{0,32},{32,64},{64,96},{1,33},{33,65},{65,97},{2,34},{34,66},{66,9... | collective-permute-start | bytes 49160 | tf_op jit(solution)/shard_map/ppermute | solution.py:641
  117.8 13.4 %collective-permute-start.11 = (f32[32,128]{1,0:T(8,128)S(1)}, f32[32,128]{1,0:T(8,128)S(1)}, u32[]{:S(2)}, u32[]{:S(2)}) collective-permute-start(f32[32,128]{1,0:T(8,128)S(1)} %get-tuple-element.53), channel_id=1, source_target_pairs={{32,0},{64,32},{96,64},{33,1},{65,33},{97,65},{34,2},{66,34},{98,6... | collective-permute-start | bytes 49160 | tf_op jit(solution)/shard_map/ppermute | solution.py:642
  127.0 5.8 %collective-permute-start.7 = (f32[32,128]{1,0:T(8,128)S(1)}, f32[32,128]{1,0:T(8,128)S(1)}, u32[]{:S(2)}, u32[]{:S(2)}) collective-permute-start(f32[32,128]{1,0:T(8,128)S(1)} %reduce_sum.28.s0), channel_id=1, source_target_pairs={{0,32},{32,64},{64,96},{96,0},{1,33},{33,65},{65,97},{97,1},{2,34}... | collective-permute-start | bytes 49160 | tf_op jit(solution)/shard_map/ppermute | solution.py:650
  127.6 5.2 %collective-permute-start.8 = (f32[32,128]{1,0:T(8,128)S(1)}, f32[32,128]{1,0:T(8,128)S(1)}, u32[]{:S(2)}, u32[]{:S(2)}) collective-permute-start(f32[32,128]{1,0:T(8,128)S(1)} %reduce_sum.28.s0), channel_id=1, source_target_pairs={{0,64},{32,96},{64,0},{96,32},{1,65},{33,97},{65,1},{97,33},{2,66}... | collective-permute-start | bytes 49160 | tf_op jit(solution)/shard_map/ppermute | solution.py:650
  131.2 2.6 %collective-permute-start.9 = (f32[32,128]{1,0:T(8,128)S(1)}, f32[32,128]{1,0:T(8,128)S(1)}, u32[]{:S(2)}, u32[]{:S(2)}) collective-permute-start(f32[32,128]{1,0:T(8,128)S(1)} %reduce_sum.28.s0), channel_id=1, source_target_pairs={{0,96},{32,0},{64,32},{96,64},{1,97},{33,1},{65,33},{97,65},{2,98}... | collective-permute-start | bytes 49160 | tf_op jit(solution)/shard_map/ppermute | solution.py:650
  137.6 16.9 %all-to-all-start.3 = ((f32[32,32,128]{2,1,0:T(8,128)}), f32[32,32,128]{2,1,0:T(8,128)S(1)}, u32[]{:S(2)}, u32[]{:S(2)}) async-start(f32[32,32,128]{2,1,0:T(8,128)} %get-tuple-element.56), calls=%async_computation.3 | async-start | bytes 1048576 | tf_op jit(solution)/shard_map/all_to_all | solution.py:643
  142.9 15.0 %collective-permute-start.15 = (f32[32,128]{1,0:T(8,128)S(1)}, f32[32,128]{1,0:T(8,128)S(1)}, u32[]{:S(2)}, u32[]{:S(2)}) collective-permute-start(f32[32,128]{1,0:T(8,128)S(1)} %get-tuple-element.59), channel_id=1, source_target_pairs={{0,32},{32,64},{64,96},{1,33},{33,65},{65,97},{2,34},{34,66},{66,9... | collective-permute-start | bytes 49160 | tf_op jit(solution)/shard_map/ppermute | solution.py:641
  144.4 13.5 %collective-permute-start.16 = (f32[32,128]{1,0:T(8,128)S(1)}, f32[32,128]{1,0:T(8,128)S(1)}, u32[]{:S(2)}, u32[]{:S(2)}) collective-permute-start(f32[32,128]{1,0:T(8,128)S(1)} %get-tuple-element.60), channel_id=1, source_target_pairs={{32,0},{64,32},{96,64},{33,1},{65,33},{97,65},{34,2},{66,34},{98,6... | collective-permute-start | bytes 49160 | tf_op jit(solution)/shard_map/ppermute | solution.py:642
  154.5 4.9 %collective-permute-start.12 = (f32[32,128]{1,0:T(8,128)S(1)}, f32[32,128]{1,0:T(8,128)S(1)}, u32[]{:S(2)}, u32[]{:S(2)}) collective-permute-start(f32[32,128]{1,0:T(8,128)S(1)} %reduce_sum.29.s0), channel_id=1, source_target_pairs={{0,32},{32,64},{64,96},{96,0},{1,33},{33,65},{65,97},{97,1},{2,34}... | collective-permute-start | bytes 49160 | tf_op jit(solution)/shard_map/ppermute | solution.py:650
  154.6 4.9 %collective-permute-start.13 = (f32[32,128]{1,0:T(8,128)S(1)}, f32[32,128]{1,0:T(8,128)S(1)}, u32[]{:S(2)}, u32[]{:S(2)}) collective-permute-start(f32[32,128]{1,0:T(8,128)S(1)} %reduce_sum.29.s0), channel_id=1, source_target_pairs={{0,64},{32,96},{64,0},{96,32},{1,65},{33,97},{65,1},{97,33},{2,66}... | collective-permute-start | bytes 49160 | tf_op jit(solution)/shard_map/ppermute | solution.py:650
  156.7 2.8 %collective-permute-start.14 = (f32[32,128]{1,0:T(8,128)S(1)}, f32[32,128]{1,0:T(8,128)S(1)}, u32[]{:S(2)}, u32[]{:S(2)}) collective-permute-start(f32[32,128]{1,0:T(8,128)S(1)} %reduce_sum.29.s0), channel_id=1, source_target_pairs={{0,96},{32,0},{64,32},{96,64},{1,97},{33,1},{65,33},{97,65},{2,98}... | collective-permute-start | bytes 49160 | tf_op jit(solution)/shard_map/ppermute | solution.py:650
  (6 other events, 85.0 us)
